TPU v7x, 512 devices: a whole 4x8x8 slice. The times are simulated.
512 devices in a mesh: dp: 8 (over z_hi, core), fsdp: 16 (over z_lo, y), tp: 4 (over x).
Axes of the slice: x: 4, y: 8, z: 8 (z_hi: 4, z_lo: 2; z = z_hi * 2 + z_lo), core: 2. Of those that a mesh axis runs over, the one named last changes fastest.
Arguments:
- layer_input: bfloat16 [65536, 4096], P(('dp', 'fsdp'), 'tp'), may hold values from -24 to 24
- value_grad: bfloat16 [65536, 2048], P(('dp', 'fsdp'), 'tp'), may hold values from -6 to 6
- residual_grad: bfloat16 [65536, 4096], P(('dp', 'fsdp'), 'tp'), may hold values from -6 to 6
- value_weight: bfloat16 [4096, 2048], P(('tp', 'fsdp')), may hold values from -0.125 to 0.125
- owner: int32 [65536, 1], P(('dp', 'fsdp')), may hold values from 0 to 15; in each aligned block of 512 rows (0 to 511, 512 to 1023, ...) at most 64 rows name the same one
- key_row: int32 [65536], P(('dp', 'fsdp')), may hold values from 0 to 255
Outputs:
- weight_grad: float32 [4096, 2048], P(('tp', 'fsdp'))
- key_grad: float32 [4096, 4096], P('fsdp', 'tp')
Inputs may be any that keep to these rules, and one draw needn't show every extreme that they name: Among the 512 tokens of one device (aligned blocks of rows) at most 64 name the same owner, and that bound is reached.
All inputs are finite; a program needn't handle non-finite values.
Results may differ from a plain program's by a relative error of at most 0.0029.
Values may be sent and summed in bfloat16 or wider, within the bound.
A program may use at most 64 MiB of HBM per device.

v0:
```python
import jax
import jax.numpy as jnp
from jax import lax
from jax.sharding import PartitionSpec as P

KEY_DEV = 256


def body(layer_input, value_grad, residual_grad, value_weight, owner, key_row):
    all_heads = lax.all_gather(value_grad, "tp", axis=1, tiled=True)
    tok_rows = layer_input.shape[0]
    features = layer_input.shape[1]
    groups = lax.axis_size("fsdp")
    slots = 2 * tok_rows // groups
    width = all_heads.shape[1]
    term = lax.dot_general(
        layer_input, all_heads, (((0,), (0,)), ((), ())), preferred_element_type=jnp.float32
    )
    pieces = term.astype(jnp.bfloat16).reshape(groups, features // groups, width)
    arrived = lax.all_to_all(pieces, "fsdp", split_axis=0, concat_axis=0, tiled=True)
    shard = jnp.sum(arrived.astype(jnp.float32), axis=0)
    back = lax.dot_general(
        all_heads,
        lax.all_gather(value_weight, "fsdp", axis=0, tiled=True),
        (((1,), (1,)), ((), ())),
        preferred_element_type=jnp.float32,
    )
    input_grad = (residual_grad.astype(jnp.float32) + back).astype(jnp.bfloat16)
    target = owner[:, 0]
    onehot = (target[:, None] == jnp.arange(groups, dtype=jnp.int32)[None, :]).astype(jnp.int32)
    position = jnp.sum(jnp.cumsum(onehot, axis=0) * onehot, axis=1) - 1
    outgoing = (
        jnp.zeros((groups, slots, features), jnp.bfloat16).at[target, position].set(input_grad)
    )
    out_keys = jnp.full((groups, slots), -1, jnp.int32).at[target, position].set(key_row)
    arrived = lax.all_to_all(outgoing, "fsdp", split_axis=0, concat_axis=0, tiled=True)
    arrived_keys = lax.all_to_all(out_keys, "fsdp", split_axis=0, concat_axis=0, tiled=True)
    flat_rows = arrived.reshape(groups * slots, features)
    selector = (
        arrived_keys.reshape(groups * slots)[:, None]
        == jnp.arange(KEY_DEV, dtype=jnp.int32)[None, :]
    ).astype(jnp.bfloat16)
    table = lax.dot_general(
        selector, flat_rows, (((0,), (0,)), ((), ())), preferred_element_type=jnp.float32
    )
    weight_grad = lax.psum(shard, "dp")
    key_grad = lax.psum(table, "dp")
    return (weight_grad, key_grad)


def solution(mesh):
    return jax.shard_map(
        body,
        mesh=mesh,
        in_specs=(
            P(("dp", "fsdp"), "tp"),
            P(("dp", "fsdp"), "tp"),
            P(("dp", "fsdp"), "tp"),
            P(("tp", "fsdp"), None),
            P(("dp", "fsdp"), None),
            P(("dp", "fsdp")),
        ),
        out_specs=(P(("tp", "fsdp"), None), P("fsdp", "tp")),
        check_vma=False,
    )
```

profile of v0, /device:TPU:1, one launch (start us, length us, event | category | flops | bytes accessed | tf_op | source)
XLA Modules:
  0.0 392.0 jit_solution(7241025913781372780)
XLA Ops:
  7.2 0.0 all-gather.3.cloned.1.call-start
  7.2 0.7 all-gather.3.cloned.1.call-update
  7.9 0.0 all-gather.5.cloned.1.call-start
  8.0 0.7 all-gather.5.cloned.1.call-update
  8.7 0.7 fusion.4
  9.4 1.1 reduce-window.6
  10.5 0.2 slice_reduce_fusion
  10.7 0.8 fusion.3
  11.5 0.7 or_select_fusion
  12.2 0.6 broadcast_in_dim.4
  12.8 71.1 %scatter_fusion = s32[16,64]{1,0:T(8,128)} fusion(s32[16,64]{1,0:T(8,128)} %broadcast_in_dim.4, s32[512]{0:T(512)S(1)} %bitcast.30, s32[512]{0:T(512)} %param.11), kind=kCustom, calls=%fused_computation | custom fusion | bytes 10240 | tf_op jit(solution)/shard_map/scatter | solution.py:35
  84.0 9.6 %all-to-all-start.1 = ((s32[16,1,64]{2,1,0:T(1,128)}), s32[16,1,64]{2,1,0:T(1,128)S(1)}, u32[]{:S(2)}, u32[]{:S(2)}) async-start(s32[16,1,64]{2,1,0:T(1,128)} %bitcast.8), calls=%async_computation.1 | async-start | bytes 16384 | tf_op jit(solution)/shard_map/all_to_all | solution.py:37
  93.6 0.0 all-gather.3.cloned.1.call-done
  93.6 6.0 %convolution_convert_fusion = bf16[1024,2048]{1,0:T(8,128)(2,1)} fusion(bf16[512,1024]{1,0:T(8,128)(2,1)S(1)} %copy-done, bf16[512,2048]{1,0:T(8,128)(2,1)} %all-gather.3.cloned.1.call-done), kind=kOutput, calls=%fused_computation.3 | convolution fusion | flops 2149580800 | bytes 7340032 | tf_op jit(solution)/shard_map/dot_general | solution.py:16
  99.6 1.3 all-to-all-done.1
  100.8 6.5 %all-to-all-start = ((bf16[16,64,2048]{2,1,0:T(8,128)(2,1)}), bf16[16,64,2048]{2,1,0:T(8,128)(2,1)}, u32[]{:S(2)}, u32[]{:S(2)}) async-start(bf16[16,64,2048]{2,1,0:T(8,128)(2,1)} %bitcast.32), calls=%async_computation | async-start | bytes 8388608 | tf_op jit(solution)/shard_map/all_to_all | solution.py:20
  107.3 50.5 %all-gather.5.cloned.1.call-done = bf16[1024,2048]{1,0:T(8,128)(2,1)} async-done(((bf16[64,2048]{1,0:T(8,128)(2,1)}), bf16[1024,2048]{1,0:T(8,128)(2,1)}) %all-gather.5.cloned.1.call-update) | async-done | bytes 4194320 | tf_op jit(solution)/shard_map/all_gather | solution.py:24
  157.8 5.2 %add_convert_fusion = bf16[512,1024]{1,0:T(8,128)(2,1)S(1)} fusion(bf16[512,1024]{1,0:T(8,128)(2,1)S(1)} %copy-done.1, bf16[512,2048]{1,0:T(8,128)(2,1)} %all-gather.3.cloned.1.call-done, bf16[1024,2048]{1,0:T(8,128)(2,1)} %all-gather.5.cloned.1.call-done), kind=kOutput, calls=%fused_computation.4 | convolution fusion | flops 2149056512 | bytes 8388608 | tf_op jit(solution)/shard_map/dot_general | solution.py:22
  163.0 1.7 broadcast_in_dim.5
  164.6 72.2 %scatter_fusion.1 = bf16[16,64,1024]{2,1,0:T(8,128)(2,1)} fusion(bf16[16,64,1024]{2,1,0:T(8,128)(2,1)} %broadcast_in_dim.5, s32[512]{0:T(512)S(1)} %bitcast.31, bf16[512,1024]{1,0:T(8,128)(2,1)S(1)} %add_convert_fusion), kind=kCustom, calls=%fused_computation.1 | custom fusion | bytes 3149824 | tf_op jit(solution)/shard_map/scatter | solution.py:33
  236.8 3.7 all-to-all-start.2
  240.6 0.0 all-reduce.3.cloned.1.call-start
  240.6 0.5 broadcast.102
  241.1 0.7 reduce.5
  241.8 0.1 eq.48
  241.9 3.8 convert_reduce_fusion
  245.7 22.4 %all-to-all-done.2 = bf16[16,64,1024]{2,1,0:T(8,128)(2,1)S(1)} async-done(((bf16[16,64,1024]{2,1,0:T(8,128)(2,1)}), bf16[16,64,1024]{2,1,0:T(8,128)(2,1)S(1)}, u32[]{:S(2)}, u32[]{:S(2)}) %all-to-all-start.2) | async-done | bytes 2097184 | tf_op jit(solution)/shard_map/all_to_all | solution.py:36
  268.0 1.9 fusion
  270.0 0.0 all-reduce.3.cloned.1.call-update
  270.0 111.2 %all-reduce.3.cloned.1.call-done = (f32[64,2048]{1,0:T(8,128)}, f32[256,1024]{1,0:T(8,128)}) async-done(((f32[64,2048]{1,0:T(8,128)}, f32[256,1024]{1,0:T(8,128)}), (f32[64,2048]{1,0:T(8,128)}, f32[256,1024]{1,0:T(8,128)})) %all-reduce.3.cloned.1.call-update) | async-done | bytes 1572880 | tf_op jit(solution)/shard_map/psum | solution.py:46
  381.3 1.9 copy.17
  383.1 2.3 copy.18
  (8 shorter events, 0.1 us)
Async XLA Ops:
  7.2 86.4 %copy-start = (bf16[512,1024]{1,0:T(8,128)(2,1)S(1)}, bf16[512,1024]{1,0:T(8,128)(2,1)}, u32[]{:S(2)}) copy-start(bf16[512,1024]{1,0:T(8,128)(2,1)} %param.6) | copy-start | bytes 3145732
  7.2 86.4 %all-gather.3.cloned.1.call-start = ((), (), s32[]{:S(2)}) async-start(), calls=%async_computation.3 | async-start | bytes 2621440 | tf_op jit(solution)/shard_map/all_gather | solution.py:10
  7.9 149.9 %all-gather.5.cloned.1.call-start = ((), (), s32[]{:S(2)}) async-start(), calls=%async_computation.4 | async-start | bytes 4456448 | tf_op jit(solution)/shard_map/all_gather | solution.py:24
  84.0 16.9 %all-to-all-start.1 = ((s32[16,1,64]{2,1,0:T(1,128)}), s32[16,1,64]{2,1,0:T(1,128)S(1)}, u32[]{:S(2)}, u32[]{:S(2)}) async-start(s32[16,1,64]{2,1,0:T(1,128)} %bitcast.8), calls=%async_computation.1 | async-start | bytes 16384 | tf_op jit(solution)/shard_map/all_to_all | solution.py:37
  100.8 56.9 %copy-start.1 = (bf16[512,1024]{1,0:T(8,128)(2,1)S(1)}, bf16[512,1024]{1,0:T(8,128)(2,1)}, u32[]{:S(2)}) copy-start(bf16[512,1024]{1,0:T(8,128)(2,1)} %param.8) | copy-start | bytes 3145732
  100.8 136.0 %all-to-all-start = ((bf16[16,64,2048]{2,1,0:T(8,128)(2,1)}), bf16[16,64,2048]{2,1,0:T(8,128)(2,1)}, u32[]{:S(2)}, u32[]{:S(2)}) async-start(bf16[16,64,2048]{2,1,0:T(8,128)(2,1)} %bitcast.32), calls=%async_computation | async-start | bytes 8388608 | tf_op jit(solution)/shard_map/all_to_all | solution.py:20
  236.8 31.2 %all-to-all-start.2 = ((bf16[16,64,1024]{2,1,0:T(8,128)(2,1)}), bf16[16,64,1024]{2,1,0:T(8,128)(2,1)S(1)}, u32[]{:S(2)}, u32[]{:S(2)}) async-start(bf16[16,64,1024]{2,1,0:T(8,128)(2,1)} %scatter_fusion.1), calls=%async_computation.2 | async-start | bytes 4194304 | tf_op jit(solution)/shard_map/all_to_all | solution.py:36
  240.6 140.7 %all-reduce.3.cloned.1.call-start = ((), (), s32[]{:S(2)}) async-start(), calls=%async_computation.5 | async-start | bytes 3145728 | tf_op jit(solution)/shard_map/psum | solution.py:46
Sparse Core Ops, SparseCore 0:
  10.1 41.4 all-gather.2
  53.6 104.1 all-gather.4
  270.1 111.0 all-reduce.2
where the time goes:
time: 396 us; the launch traced here: 392 us
  waiting for transfers between devices  187 us (47%)
  local copies, waits for them, and re-layouts  151 us (38%)
  starting transfers between devices  19.9 us (5%)
  between operations  13.8 us (3%)
  matrix products  13.1 us (3%)
  other arithmetic  7.81 us (2%)
    psum x1, waiting for transfers between devices, body(): weight_grad = lax.psum(shard, 'dp')  111 us
    scatter x1, local copies, waits for them, and re-layouts, body(): jnp.zeros((groups, slots, features), jnp.bfloat16).at[target, position]  72.2 us
    scatter x1, local copies, waits for them, and re-layouts, body(): jnp.full((groups, slots), -1, jnp.int32).at[target, position].set(key_row)  71.1 us
    all_gather x1, waiting for transfers between devices, body(): lax.all_gather(value_weight, 'fsdp', axis=0, tiled=True)  50.5 us
    all_to_all x1, waiting for transfers between devices, body(): lax.all_to_all(outgoing, 'fsdp', split_axis=0, concat_axis=0, tiled=True)  22.4 us
    all_to_all x1, starting transfers between devices, body(): lax.all_to_all(out_keys, 'fsdp', split_axis=0, concat_axis=0, tiled=True)  9.6 us
  transfers between devices with their start and end apart: 6, of which 4 were waited for; matrix products, arithmetic and copies ran while one was open for 42% of the time, Pallas kernels for 0%

commit v1 on v0

--- a/solution.py
+++ b/solution.py
@@ -4,6 +4,13 @@
 from jax.sharding import PartitionSpec as P
 
 KEY_DEV = 256
+
+
+def choose_the_side(slab_in):
+    return jnp.concatenate(
+        jax.lax.all_to_all(jnp.stack(jax.lax.axis_size("fsdp") * [slab_in], axis=0), "fsdp", 0, 0),
+        axis=0,
+    )
 
 
 def body(layer_input, value_grad, residual_grad, value_weight, owner, key_row):
@@ -21,7 +28,7 @@
     shard = jnp.sum(arrived.astype(jnp.float32), axis=0)
     back = lax.dot_general(
         all_heads,
-        lax.all_gather(value_weight, "fsdp", axis=0, tiled=True),
+        choose_the_side(value_weight),
         (((1,), (1,)), ((), ())),
         preferred_element_type=jnp.float32,
     )

time: 396 us -> 438 us (1.11)
  waiting for transfers between devices: 187 us -> 236 us
  local copies, waits for them, and re-layouts: 151 us -> 125 us
  blocking collectives: 0 us -> 16.7 us
    all_gather x1 -> x0, waiting for transfers between devices: 50.5 us -> none  [body(): lax.all_gather(value_weight, 'fsdp', axis=0, tiled=True)]
    all_to_all x1, waiting for transfers between devices: 1.26 us -> 44.9 us  [choose_the_side(): jax.lax.all_to_all(jnp.stack(jax.lax.axis_size('fsdp') * [slab_in], axis=...]
    all_gather x1, waiting for transfers between devices: 0.02 us -> 43.2 us  [body(): all_heads = lax.all_gather(value_grad, 'tp', axis=1, tiled=True)]
    scatter x1, local copies, waits for them, and re-layouts: 71.1 us -> 43.2 us  [body(): jnp.full((groups, slots), -1, jnp.int32).at[target, position].set(key_row)]
    psum x1, waiting for transfers between devices: 111 us -> 88.7 us  [body(): weight_grad = lax.psum(shard, 'dp')]
    all_to_all x1, waiting for transfers between devices: 22.4 us -> 42.8 us  [body(): lax.all_to_all(outgoing, 'fsdp', split_axis=0, concat_axis=0, tiled=True)]
    all_to_all x0 -> x1, blocking collectives: none -> 16.7 us  [body(): lax.all_to_all(out_keys, 'fsdp', split_axis=0, concat_axis=0, tiled=True)]
    all_to_all x1, waiting for transfers between devices: 0.01 us -> 15.7 us  [body(): lax.all_to_all(pieces, 'fsdp', split_axis=0, concat_axis=0, tiled=True)]
  transfers between devices with their start and end apart: 6 -> 5, of which waited for: 4 -> 5; matrix products, arithmetic and copies ran while one was open for 42% -> 21% of each run, Pallas kernels for 0% -> 0%
where the time goes in v1:
time: 438 us; the launch traced here: 434 us
  waiting for transfers between devices  236 us (54%)
  local copies, waits for them, and re-layouts  125 us (29%)
  starting transfers between devices  22.3 us (5%)
  blocking collectives  16.7 us (4%)
  between operations  14.1 us (3%)
  matrix products  13 us (3%)
  other arithmetic  7.9 us (2%)
    psum x1, waiting for transfers between devices, body(): weight_grad = lax.psum(shard, 'dp')  88.7 us
    scatter x1, local copies, waits for them, and re-layouts, body(): jnp.zeros((groups, slots, features), jnp.bfloat16).at[target, position]  72.2 us
    all_to_all x1, waiting for transfers between devices, choose_the_side(): jax.lax.all_to_all(jnp.stack(jax.lax.axis_size('fsdp') * [slab_in], axis=...  44.9 us
    scatter x1, local copies, waits for them, and re-layouts, body(): jnp.full((groups, slots), -1, jnp.int32).at[target, position].set(key_row)  43.2 us
    all_gather x1, waiting for transfers between devices, body(): all_heads = lax.all_gather(value_grad, 'tp', axis=1, tiled=True)  43.2 us
    all_to_all x1, waiting for transfers between devices, body(): lax.all_to_all(outgoing, 'fsdp', split_axis=0, concat_axis=0, tiled=True)  42.8 us
    all_to_all x1, blocking collectives, body(): lax.all_to_all(out_keys, 'fsdp', split_axis=0, concat_axis=0, tiled=True)  16.7 us
    all_to_all x1, waiting for transfers between devices, body(): lax.all_to_all(pieces, 'fsdp', split_axis=0, concat_axis=0, tiled=True)  15.7 us
  transfers between devices with their start and end apart: 5, of which 5 were waited for; matrix products, arithmetic and copies ran while one was open for 21% of the time, Pallas kernels for 0%

profile of v1, /device:TPU:1, one launch (start us, length us, event | category | flops | bytes accessed | tf_op | source)
XLA Modules:
  0.0 434.5 jit_solution(8110806374919963127)
XLA Ops:
  7.2 0.0 copy-start
  7.2 0.8 fusion.4
  8.0 1.1 reduce-window.6
  9.1 0.2 slice_reduce_fusion
  9.3 0.8 fusion.3
  10.1 0.7 or_select_fusion
  10.9 43.2 %scatter_fusion = s32[16,64]{1,0:T(8,128)S(1)} fusion(s32[16,64]{1,0:T(8,128)S(1)} %broadcast_in_dim.4, s32[512]{0:T(512)S(1)} %bitcast.32, s32[512]{0:T(512)} %param.11), kind=kCustom, calls=%fused_computation | custom fusion | bytes 10240 | tf_op jit(solution)/shard_map/scatter | solution.py:42
  54.1 16.7 %all_to_all.24 = s32[16,1,64]{2,1,0:T(1,128)S(1)} all-to-all(s32[16,1,64]{2,1,0:T(1,128)S(1)} %bitcast.31), channel_id=1, replica_groups=mesh['dp'=8,'fsdp'=16,'tp'=4] {'fsdp'}, dimensions={0} | all-to-all | bytes 8192 | tf_op jit(solution)/shard_map/all_to_all | solution.py:44
  70.8 2.5 stack.2
  73.3 4.5 %all-to-all-start.2 = ((bf16[16,64,2048]{2,1,0:T(8,128)(2,1)}), bf16[16,64,2048]{2,1,0:T(8,128)(2,1)}, u32[]{:S(2)}, u32[]{:S(2)}) async-start(bf16[16,64,2048]{2,1,0:T(8,128)(2,1)} %stack.2), calls=%async_computation.2 | async-start | bytes 8388608 | tf_op jit(solution)/shard_map/all_to_all | solution.py:11
  77.8 0.0 all-gather.2.cloned.1.call-start
  77.9 0.7 all-gather.2.cloned.1.call-update
  78.6 43.2 %all-gather.2.cloned.1.call-done = bf16[512,2048]{1,0:T(8,128)(2,1)} async-done(((bf16[512,512]{1,0:T(8,128)(2,1)}), bf16[512,2048]{1,0:T(8,128)(2,1)}) %all-gather.2.cloned.1.call-update) | async-done | bytes 2097168 | tf_op jit(solution)/shard_map/all_gather | solution.py:17
  121.8 5.9 %convolution_convert_fusion = bf16[1024,2048]{1,0:T(8,128)(2,1)} fusion(bf16[512,1024]{1,0:T(8,128)(2,1)S(1)} %copy-done, bf16[512,2048]{1,0:T(8,128)(2,1)} %all-gather.2.cloned.1.call-done), kind=kOutput, calls=%fused_computation.3 | convolution fusion | flops 2149580800 | bytes 7340032 | tf_op jit(solution)/shard_map/dot_general | solution.py:23
  127.7 44.9 %all-to-all-done.2 = bf16[16,64,2048]{2,1,0:T(8,128)(2,1)} async-done(((bf16[16,64,2048]{2,1,0:T(8,128)(2,1)}), bf16[16,64,2048]{2,1,0:T(8,128)(2,1)}, u32[]{:S(2)}, u32[]{:S(2)}) %all-to-all-start.2) | async-done | bytes 4194336 | tf_op jit(solution)/shard_map/all_to_all | solution.py:11
  172.6 8.9 %all-to-all-start = ((bf16[16,64,2048]{2,1,0:T(8,128)(2,1)}), bf16[16,64,2048]{2,1,0:T(8,128)(2,1)}, u32[]{:S(2)}, u32[]{:S(2)}) async-start(bf16[16,64,2048]{2,1,0:T(8,128)(2,1)} %bitcast.34), calls=%async_computation | async-start | bytes 8388608 | tf_op jit(solution)/shard_map/all_to_all | solution.py:27
  181.5 5.2 %add_convert_fusion = bf16[512,1024]{1,0:T(8,128)(2,1)S(1)} fusion(bf16[512,1024]{1,0:T(8,128)(2,1)S(1)} %copy-done.2, bf16[512,2048]{1,0:T(8,128)(2,1)} %all-gather.2.cloned.1.call-done, bf16[1024,2048]{1,0:T(8,128)(2,1)} %bitcast.9), kind=kOutput, calls=%fused_computation.4 | convolution fusion | flops 2149056512 | bytes 8388608 | tf_op jit(solution)/shard_map/dot_general | solution.py:29
  186.7 1.7 broadcast_in_dim.5
  188.4 72.2 %scatter_fusion.1 = bf16[16,64,1024]{2,1,0:T(8,128)(2,1)} fusion(bf16[16,64,1024]{2,1,0:T(8,128)(2,1)} %broadcast_in_dim.5, s32[512]{0:T(512)S(1)} %bitcast.33, bf16[512,1024]{1,0:T(8,128)(2,1)S(1)} %add_convert_fusion), kind=kCustom, calls=%fused_computation.1 | custom fusion | bytes 3149824 | tf_op jit(solution)/shard_map/scatter | solution.py:40
  260.6 15.7 %all-to-all-done = bf16[16,64,2048]{2,1,0:T(8,128)(2,1)} async-done(((bf16[16,64,2048]{2,1,0:T(8,128)(2,1)}), bf16[16,64,2048]{2,1,0:T(8,128)(2,1)}, u32[]{:S(2)}, u32[]{:S(2)}) %all-to-all-start) | async-done | bytes 4194336 | tf_op jit(solution)/shard_map/all_to_all | solution.py:27
  276.3 8.7 %all-to-all-start.3 = ((bf16[16,64,1024]{2,1,0:T(8,128)(2,1)}), bf16[16,64,1024]{2,1,0:T(8,128)(2,1)S(1)}, u32[]{:S(2)}, u32[]{:S(2)}) async-start(bf16[16,64,1024]{2,1,0:T(8,128)(2,1)} %scatter_fusion.1), calls=%async_computation.3 | async-start | bytes 4194304 | tf_op jit(solution)/shard_map/all_to_all | solution.py:43
  285.0 0.0 all-reduce.3.cloned.1.call-start
  285.0 0.5 broadcast.104
  285.5 0.7 reduce.5
  286.2 0.1 eq.48
  286.3 3.8 convert_reduce_fusion
  290.1 42.8 %all-to-all-done.3 = bf16[16,64,1024]{2,1,0:T(8,128)(2,1)S(1)} async-done(((bf16[16,64,1024]{2,1,0:T(8,128)(2,1)}), bf16[16,64,1024]{2,1,0:T(8,128)(2,1)S(1)}, u32[]{:S(2)}, u32[]{:S(2)}) %all-to-all-start.3) | async-done | bytes 2097184 | tf_op jit(solution)/shard_map/all_to_all | solution.py:43
  332.8 1.9 fusion
  334.8 0.0 all-reduce.3.cloned.1.call-update
  334.8 88.7 %all-reduce.3.cloned.1.call-done = (f32[64,2048]{1,0:T(8,128)}, f32[256,1024]{1,0:T(8,128)}) async-done(((f32[64,2048]{1,0:T(8,128)}, f32[256,1024]{1,0:T(8,128)}), (f32[64,2048]{1,0:T(8,128)}, f32[256,1024]{1,0:T(8,128)})) %all-reduce.3.cloned.1.call-update) | async-done | bytes 1572880 | tf_op jit(solution)/shard_map/psum | solution.py:53
  423.5 1.9 copy.17
  425.3 2.3 copy.18
  (9 shorter events, 0.1 us)
Async XLA Ops:
  7.2 114.6 %copy-start = (bf16[512,1024]{1,0:T(8,128)(2,1)S(1)}, bf16[512,1024]{1,0:T(8,128)(2,1)}, u32[]{:S(2)}) copy-start(bf16[512,1024]{1,0:T(8,128)(2,1)} %param.6) | copy-start | bytes 3145732
  10.8 59.9 %copy-start.1 = (bf16[64,2048]{1,0:T(8,128)(2,1)S(1)}, bf16[64,2048]{1,0:T(8,128)(2,1)}, u32[]{:S(2)}) copy-start(bf16[64,2048]{1,0:T(8,128)(2,1)} %param.9) | copy-start | bytes 786436
  73.3 99.3 %all-to-all-start.2 = ((bf16[16,64,2048]{2,1,0:T(8,128)(2,1)}), bf16[16,64,2048]{2,1,0:T(8,128)(2,1)}, u32[]{:S(2)}, u32[]{:S(2)}) async-start(bf16[16,64,2048]{2,1,0:T(8,128)(2,1)} %stack.2), calls=%async_computation.2 | async-start | bytes 8388608 | tf_op jit(solution)/shard_map/all_to_all | solution.py:11
  77.8 43.9 %all-gather.2.cloned.1.call-start = ((), (), s32[]{:S(2)}) async-start(), calls=%async_computation.4 | async-start | bytes 2621440 | tf_op jit(solution)/shard_map/all_gather | solution.py:17
  172.6 9.0 %copy-start.2 = (bf16[512,1024]{1,0:T(8,128)(2,1)S(1)}, bf16[512,1024]{1,0:T(8,128)(2,1)}, u32[]{:S(2)}) copy-start(bf16[512,1024]{1,0:T(8,128)(2,1)} %param.8) | copy-start | bytes 3145732
  172.6 103.7 %all-to-all-start = ((bf16[16,64,2048]{2,1,0:T(8,128)(2,1)}), bf16[16,64,2048]{2,1,0:T(8,128)(2,1)}, u32[]{:S(2)}, u32[]{:S(2)}) async-start(bf16[16,64,2048]{2,1,0:T(8,128)(2,1)} %bitcast.34), calls=%async_computation | async-start | bytes 8388608 | tf_op jit(solution)/shard_map/all_to_all | solution.py:27
  276.3 56.6 %all-to-all-start.3 = ((bf16[16,64,1024]{2,1,0:T(8,128)(2,1)}), bf16[16,64,1024]{2,1,0:T(8,128)(2,1)S(1)}, u32[]{:S(2)}, u32[]{:S(2)}) async-start(bf16[16,64,1024]{2,1,0:T(8,128)(2,1)} %scatter_fusion.1), calls=%async_computation.3 | async-start | bytes 4194304 | tf_op jit(solution)/shard_map/all_to_all | solution.py:43
  285.0 138.5 %all-reduce.3.cloned.1.call-start = ((), (), s32[]{:S(2)}) async-start(), calls=%async_computation.5 | async-start | bytes 3145728 | tf_op jit(solution)/shard_map/psum | solution.py:53
Sparse Core Ops, SparseCore 0:
  80.7 40.9 all-gather.1
  334.9 88.4 all-reduce.2
